TPU v7x, 128 devices: a whole 4x4x4 slice. The times are simulated.
128 devices in a mesh: probe: 4 (over z_hi, core), sx: 4 (over x), sy: 8 (over y, z_lo).
Axes of the slice: x: 4, y: 4, z: 4 (z_hi: 2, z_lo: 2; z = z_hi * 2 + z_lo), core: 2. Of those that a mesh axis runs over, the one named last changes fastest.
Arguments:
- probes: float32 [8, 128, 256, 256], P('probe', 'sx', 'sy'), may hold values from -6 to 6
- velocity: float32 [3, 128, 256, 256], P(None, 'sx', 'sy'), may hold values from -0.15 to 0.15
- diffusivity: float32 [128, 256, 256], P('sx', 'sy'), may hold values from 0.02 to 0.15
- obs_weight: float32 [128, 256, 256], P('sx', 'sy'), may hold values from 0.05 to 1
Outputs:
- basis_fields: float32 [8, 128, 256, 256], P('probe', 'sx', 'sy')
- projected_hessian: float32 [8, 8], replicated
All inputs are finite; a program needn't handle non-finite values.
Results may differ from a plain program's by a relative error of at most 0.00013.
Values sent between devices are 32-bit elements; how exact they have to be, the bound alone decides.
A program may use at most 128 MiB of HBM per device.

v0:
```python
import jax
import jax.numpy as jnp
from jax import lax
from jax.sharding import PartitionSpec as P

STEPS = 4


def extended(value, sides, width):
    for axis, dim in sides:
        devices, length = (lax.axis_size(axis), value.shape[dim])
        up = [(i, (i + 1) % devices) for i in range(devices - 1)]
        down = [(j, i) for i, j in up]
        last = lax.slice_in_dim(value, length - width, length, axis=dim)
        leading = lax.slice_in_dim(value, 0, width, axis=dim)
        before = lax.ppermute(last, axis, up)
        after = lax.ppermute(leading, axis, down)
        value = jnp.concatenate([before, value, after], axis=dim)
    return value


def forward_step(state, coeffs):
    cc = coeffs[:, 1:-1, 1:-1, :]
    spread = cc[0]
    inner = state[:, 1:-1, 1:-1, :]
    padded = jnp.pad(inner, ((0, 0), (0, 0), (0, 0), (1, 1)))
    result = (1.0 - 6.0 * spread) * inner
    result = (
        result
        + (spread - 0.5 * cc[1]) * state[:, 2:, 1:-1, :]
        + (spread + 0.5 * cc[1]) * state[:, :-2, 1:-1, :]
    )
    result = (
        result
        + (spread - 0.5 * cc[2]) * state[:, 1:-1, 2:, :]
        + (spread + 0.5 * cc[2]) * state[:, 1:-1, :-2, :]
    )
    result = (
        result
        + (spread - 0.5 * cc[3]) * padded[..., 2:]
        + (spread + 0.5 * cc[3]) * padded[..., :-2]
    )
    return result


def adjoint_step(state, coeffs):
    spread = coeffs[0]
    plus_x = (spread - 0.5 * coeffs[1]) * state
    minus_x = (spread + 0.5 * coeffs[1]) * state
    plus_y = (spread - 0.5 * coeffs[2]) * state
    minus_y = (spread + 0.5 * coeffs[2]) * state
    cc = coeffs[:, 1:-1, 1:-1, :]
    inner = state[:, 1:-1, 1:-1, :]
    pad_plus = jnp.pad((cc[0] - 0.5 * cc[3]) * inner, ((0, 0), (0, 0), (0, 0), (1, 1)))
    pad_minus = jnp.pad((cc[0] + 0.5 * cc[3]) * inner, ((0, 0), (0, 0), (0, 0), (1, 1)))
    result = (1.0 - 6.0 * cc[0]) * inner
    result = result + plus_x[:, :-2, 1:-1, :] + minus_x[:, 2:, 1:-1, :]
    result = result + plus_y[:, 1:-1, :-2, :] + minus_y[:, 1:-1, 2:, :]
    result = result + pad_plus[..., :-2] + pad_minus[..., 2:]
    return result


def factor_inverse(gram, count):
    lower = jnp.linalg.cholesky(gram)
    return jax.scipy.linalg.solve_triangular(lower, jnp.eye(count, dtype=jnp.float32), lower=True)


def shards(probes, velocity, diffusivity, obs_weight):
    group = probes.shape[0]
    count = group * lax.axis_size("probe")
    ncells = (
        probes.shape[1]
        * probes.shape[2]
        * probes.shape[3]
        * lax.axis_size("sx")
        * lax.axis_size("sy")
    )
    coeffs = jnp.concatenate([diffusivity[None], velocity], axis=0)
    highest = lax.Precision.HIGHEST
    edge_coeffs = extended(coeffs, (("sx", 1), ("sy", 2)), 1)

    def forward(state):
        for step in range(STEPS):
            padded = extended(state, (("sx", 1), ("sy", 2)), 1)
            state = forward_step(padded, edge_coeffs)
        return state

    state = obs_weight * forward(probes)
    for step in range(STEPS):
        padded = extended(state, (("sx", 1), ("sy", 2)), 1)
        state = adjoint_step(padded, edge_coeffs)
    images = state
    again = forward(images)
    root = jnp.sqrt(obs_weight) * again
    both = jnp.stack([images, root], axis=1)
    slabs = lax.all_to_all(both, "probe", split_axis=2, concat_axis=0, tiled=True)
    flat = slabs[:, 0].reshape(count, -1)
    flat_root = slabs[:, 1].reshape(count, -1)
    partial_gram = jnp.dot(flat, flat.T, precision=highest)
    partial_cross = jnp.dot(flat_root, flat_root.T, precision=highest)
    sums = lax.psum(jnp.stack([partial_gram, partial_cross]), ("probe", "sx", "sy")) / ncells
    gram, cross = (sums[0], sums[1])
    inverse = factor_inverse(gram, count)
    basis_slab = jnp.dot(inverse, flat, precision=highest)
    basis_fields = lax.all_to_all(
        basis_slab.reshape(slabs[:, 0].shape), "probe", split_axis=0, concat_axis=1, tiled=True
    )
    projected = jnp.dot(jnp.dot(inverse, cross, precision=highest), inverse.T, precision=highest)
    return (basis_fields, projected)


def solution(mesh):
    return jax.shard_map(
        shards,
        mesh=mesh,
        in_specs=(
            P("probe", "sx", "sy", None),
            P(None, "sx", "sy", None),
            P("sx", "sy", None),
            P("sx", "sy", None),
        ),
        out_specs=(P("probe", "sx", "sy", None), P()),
        check_vma=False,
    )
```

profile of v0, /device:TPU:1, one launch (start us, length us, event | category | flops | bytes accessed | tf_op | source)
XLA Modules:
  0.0 471.6 jit_solution(13638757533432052887)
XLA Ops:
  3.0 4.6 collective-permute-start.1
  12.0 4.4 collective-permute-start.3
  21.8 3.5 fusion.10
  26.7 4.0 collective-permute-start.5
  33.3 4.9 %collective-permute-start.7 = (f32[2,34,1,256]{3,1,2,0:T(8,128)S(1)}, f32[2,34,1,256]{3,1,2,0:T(8,128)S(1)}, u32[]{:S(2)}, u32[]{:S(2)}) collective-permute-start(f32[2,34,1,256]{3,1,2,0:T(8,128)S(1)} %get-tuple-element.46), channel_id=1, source_target_pairs={{0,1},{1,2},{2,3},{3,4},{4,5},{5,6},{6,7},{8,9},{9,10},{10,11},{11... | collective-permute-start | bytes 208904 | tf_op jit(solution)/shard_map/ppermute | solution.py:16
  38.3 4.0 collective-permute-start.16
  43.6 3.5 fusion.14
  48.4 4.6 collective-permute-start.9
  53.3 4.4 collective-permute-start.18
  60.4 4.8 %collective-permute-start.11 = (f32[2,34,1,256]{3,1,2,0:T(8,128)S(1)}, f32[2,34,1,256]{3,1,2,0:T(8,128)S(1)}, u32[]{:S(2)}, u32[]{:S(2)}) collective-permute-start(f32[2,34,1,256]{3,1,2,0:T(8,128)S(1)} %get-tuple-element.44), channel_id=1, source_target_pairs={{0,1},{1,2},{2,3},{3,4},{4,5},{5,6},{6,7},{8,9},{9,10},{10,11},{11... | collective-permute-start | bytes 208904 | tf_op jit(solution)/shard_map/ppermute | solution.py:16
  68.3 3.4 fusion.18
  73.1 4.3 collective-permute-start.13
  80.0 4.4 collective-permute-start.15
  85.9 3.5 broadcast_multiply_fusion.3
  89.6 3.7 collective-permute-start.20
  98.3 4.3 collective-permute-start.22
  105.5 3.5 collective-permute-done.23
  109.5 3.9 broadcast_multiply_fusion.2
  113.5 3.5 collective-permute-start.24
  118.4 3.7 collective-permute-done.25
  122.1 4.3 collective-permute-start.26
  132.0 3.9 broadcast_multiply_fusion.1
  140.7 3.9 collective-permute-done.29
  149.4 3.5 collective-permute-done.31
  153.3 3.7 broadcast_multiply_fusion
  161.4 3.7 collective-permute-done.33
  165.1 4.3 collective-permute-start.34
  171.1 3.4 collective-permute-done.35
  179.1 4.0 collective-permute-start.37
  185.8 4.0 collective-permute-start.39
  192.0 3.4 fusion.27
  196.8 4.0 collective-permute-start.41
  203.5 4.4 collective-permute-start.43
  210.5 3.4 fusion.31
  215.3 4.4 collective-permute-start.45
  222.4 4.4 collective-permute-start.47
  233.2 4.6 collective-permute-start.49
  240.4 5.3 %collective-permute-start.51 = (f32[2,34,1,256]{3,1,2,0:T(8,128)S(1)}, f32[2,34,1,256]{3,1,2,0:T(8,128)S(1)}, u32[]{:S(2)}, u32[]{:S(2)}) collective-permute-start(f32[2,34,1,256]{3,1,2,0:T(8,128)S(1)} %get-tuple-element.26), channel_id=1, source_target_pairs={{0,1},{1,2},{2,3},{3,4},{4,5},{5,6},{6,7},{8,9},{9,10},{10,11},{11... | collective-permute-start | bytes 208904 | tf_op jit(solution)/shard_map/ppermute | solution.py:16
  247.1 3.5 fusion.41
  253.3 79.6 %all_to_all.36 = f32[2,2,32,32,256]{4,3,0,1,2:T(8,128)S(1)} all-to-all(f32[2,2,32,32,256]{4,3,0,1,2:T(8,128)S(1)} %copy.58), channel_id=1, replica_groups=mesh['probe'=4,'sx'=4,'sy'=8] {'probe'}, dimensions={2} | all-to-all | bytes 8388608 | tf_op jit(solution)/shard_map/all_to_all | solution.py:96
  333.0 5.2 %copy.72 = f32[2,2,4,8,32,256]{5,0,2,4,3,1:T(2,128)} copy(f32[2,2,4,8,32,256]{5,4,0,1,3,2:T(8,128)S(1)} %bitcast.90) | data formatting | bytes 8388608 | tf_op jit(solution)/shard_map/all_to_all | solution.py:96
  338.2 6.1 %all_to_all.29 = f32[8,2,8,32,256]{4,0,3,2,1:T(8,128)} reshape(f32[4,2,2,8,32,256]{5,1,0,4,3,2:T(2,128)} %bitcast.91) | data formatting | bytes 8388608 | tf_op jit(solution)/shard_map/all_to_all | solution.py:96
  344.4 7.1 %fusion.131 = f32[1,8,8]{2,1,0:T(8,128)S(1)} fusion(f32[8,2,8,32,256]{4,0,3,2,1:T(8,128)} %all_to_all.29), kind=kOutput, calls=%fused_computation.253 | convolution fusion | flops 50331648 | bytes 2097408 | tf_op jit(solution)/shard_map/dot_general | solution.py:99
  351.5 7.1 %fusion.134 = f32[1,8,8]{2,1,0:T(8,128)S(1)} fusion(f32[8,2,8,32,256]{4,0,3,2,1:T(8,128)} %all_to_all.29), kind=kOutput, calls=%fused_computation.254 | convolution fusion | flops 50331648 | bytes 2097408 | tf_op jit(solution)/shard_map/dot_general | solution.py:100
  358.6 72.6 %psum.7 = f32[2,8,8]{2,1,0:T(8,128)S(1)} all-reduce(f32[2,8,8]{2,1,0:T(8,128)S(1)} %pad_maximum_fusion.117), channel_id=1, replica_groups=mesh['probe'=4,'sx'=4,'sy'=8] {'probe','sx','sy'}, use_global_device_ids=true, to_apply=%region_0.1 | all-reduce | flops 128 | bytes 1024 | tf_op jit(solution)/shard_map/psum | solution.py:101
  434.2 3.4 fusion.124
  439.6 4.1 all-to-all-start.1
  444.6 25.3 %all-to-all-done.1 = f32[8,8,32,256]{3,2,1,0:T(8,128)S(1)} async-done(((f32[8,8,32,256]{3,2,1,0:T(8,128)}), f32[8,8,32,256]{3,2,1,0:T(8,128)S(1)}, u32[]{:S(2)}, u32[]{:S(2)}) %all-to-all-start.1) | async-done | bytes 2097184 | tf_op jit(solution)/shard_map/all_to_all | solution.py:105
  (167 shorter events, 101.8 us)
Async XLA Ops:
  1.6 8.9 %collective-permute-start = (f32[2,1,32,256]{3,1,2,0:T(1,128)S(1)}, f32[2,1,32,256]{3,1,2,0:T(1,128)S(1)}, u32[]{:S(2)}, u32[]{:S(2)}) collective-permute-start(f32[2,1,32,256]{3,1,2,0:T(1,128)S(1)} %copy.38), channel_id=1, source_target_pairs={{8,0},{16,8},{24,16},{9,1},{17,9},{25,17},{10,2},{18,10},{26,18},{... | collective-permute-start | bytes 196616 | tf_op jit(solution)/shard_map/ppermute | solution.py:17
  3.0 7.6 %collective-permute-start.1 = (f32[2,1,32,256]{3,1,2,0:T(1,128)S(1)}, f32[2,1,32,256]{3,1,2,0:T(1,128)S(1)}, u32[]{:S(2)}, u32[]{:S(2)}) collective-permute-start(f32[2,1,32,256]{3,1,2,0:T(1,128)S(1)} %copy.41), channel_id=1, source_target_pairs={{0,8},{8,16},{16,24},{1,9},{9,17},{17,25},{2,10},{10,18},{18,26},{... | collective-permute-start | bytes 196616 | tf_op jit(solution)/shard_map/ppermute | solution.py:16
  10.6 11.2 %collective-permute-start.2 = (f32[2,34,1,256]{3,1,2,0:T(8,128)S(1)}, f32[2,34,1,256]{3,1,2,0:T(8,128)S(1)}, u32[]{:S(2)}, u32[]{:S(2)}) collective-permute-start(f32[2,34,1,256]{3,1,2,0:T(8,128)S(1)} %get-tuple-element.47), channel_id=1, source_target_pairs={{1,0},{2,1},{3,2},{4,3},{5,4},{6,5},{7,6},{9,8},{10,9},{11,10},{12... | collective-permute-start | bytes 208904 | tf_op jit(solution)/shard_map/ppermute | solution.py:17
  12.0 9.8 %collective-permute-start.3 = (f32[2,34,1,256]{3,1,2,0:T(8,128)S(1)}, f32[2,34,1,256]{3,1,2,0:T(8,128)S(1)}, u32[]{:S(2)}, u32[]{:S(2)}) collective-permute-start(f32[2,34,1,256]{3,1,2,0:T(8,128)S(1)} %get-tuple-element.48), channel_id=1, source_target_pairs={{0,1},{1,2},{2,3},{3,4},{4,5},{5,6},{6,7},{8,9},{9,10},{10,11},{11... | collective-permute-start | bytes 208904 | tf_op jit(solution)/shard_map/ppermute | solution.py:16
  25.4 5.3 %collective-permute-start.4 = (f32[2,1,32,256]{3,1,2,0:T(1,128)S(1)}, f32[2,1,32,256]{3,1,2,0:T(1,128)S(1)}, u32[]{:S(2)}, u32[]{:S(2)}) collective-permute-start(f32[2,1,32,256]{3,1,2,0:T(1,128)S(1)} %get-tuple-element.70), channel_id=1, source_target_pairs={{8,0},{16,8},{24,16},{9,1},{17,9},{25,17},{10,2},{18,10},{26,18},{... | collective-permute-start | bytes 196616 | tf_op jit(solution)/shard_map/ppermute | solution.py:17
  26.7 5.3 %collective-permute-start.5 = (f32[2,1,32,256]{3,1,2,0:T(1,128)S(1)}, f32[2,1,32,256]{3,1,2,0:T(1,128)S(1)}, u32[]{:S(2)}, u32[]{:S(2)}) collective-permute-start(f32[2,1,32,256]{3,1,2,0:T(1,128)S(1)} %get-tuple-element.69), channel_id=1, source_target_pairs={{0,8},{8,16},{16,24},{1,9},{9,17},{17,25},{2,10},{10,18},{18,26},{... | collective-permute-start | bytes 196616 | tf_op jit(solution)/shard_map/ppermute | solution.py:16
  32.0 11.5 %collective-permute-start.6 = (f32[2,34,1,256]{3,1,2,0:T(8,128)S(1)}, f32[2,34,1,256]{3,1,2,0:T(8,128)S(1)}, u32[]{:S(2)}, u32[]{:S(2)}) collective-permute-start(f32[2,34,1,256]{3,1,2,0:T(8,128)S(1)} %get-tuple-element.45), channel_id=1, source_target_pairs={{1,0},{2,1},{3,2},{4,3},{5,4},{6,5},{7,6},{9,8},{10,9},{11,10},{12... | collective-permute-start | bytes 208904 | tf_op jit(solution)/shard_map/ppermute | solution.py:17
  33.3 10.2 %collective-permute-start.7 = (f32[2,34,1,256]{3,1,2,0:T(8,128)S(1)}, f32[2,34,1,256]{3,1,2,0:T(8,128)S(1)}, u32[]{:S(2)}, u32[]{:S(2)}) collective-permute-start(f32[2,34,1,256]{3,1,2,0:T(8,128)S(1)} %get-tuple-element.46), channel_id=1, source_target_pairs={{0,1},{1,2},{2,3},{3,4},{4,5},{5,6},{6,7},{8,9},{9,10},{10,11},{11... | collective-permute-start | bytes 208904 | tf_op jit(solution)/shard_map/ppermute | solution.py:16
  38.3 14.8 %collective-permute-start.16 = (f32[4,1,32,256]{3,2,1,0:T(8,128)S(1)}, f32[4,1,32,256]{3,2,1,0:T(8,128)S(1)}, u32[]{:S(2)}, u32[]{:S(2)}) collective-permute-start(f32[4,1,32,256]{3,2,1,0:T(8,128)S(1)} %get-tuple-element.17), channel_id=1, source_target_pairs={{0,8},{8,16},{16,24},{1,9},{9,17},{17,25},{2,10},{10,18},{18,26},{... | collective-permute-start | bytes 393224 | tf_op jit(solution)/shard_map/ppermute | solution.py:16
  42.3 10.8 %collective-permute-start.17 = (f32[4,1,32,256]{3,2,1,0:T(8,128)S(1)}, f32[4,1,32,256]{3,2,1,0:T(8,128)S(1)}, u32[]{:S(2)}, u32[]{:S(2)}) collective-permute-start(f32[4,1,32,256]{3,2,1,0:T(8,128)S(1)} %get-tuple-element.18), channel_id=1, source_target_pairs={{8,0},{16,8},{24,16},{9,1},{17,9},{25,17},{10,2},{18,10},{26,18},{... | collective-permute-start | bytes 393224 | tf_op jit(solution)/shard_map/ppermute | solution.py:17
  47.1 11.9 %collective-permute-start.8 = (f32[2,1,32,256]{3,1,2,0:T(1,128)S(1)}, f32[2,1,32,256]{3,1,2,0:T(1,128)S(1)}, u32[]{:S(2)}, u32[]{:S(2)}) collective-permute-start(f32[2,1,32,256]{3,1,2,0:T(1,128)S(1)} %get-tuple-element.68), channel_id=1, source_target_pairs={{8,0},{16,8},{24,16},{9,1},{17,9},{25,17},{10,2},{18,10},{26,18},{... | collective-permute-start | bytes 196616 | tf_op jit(solution)/shard_map/ppermute | solution.py:17
  48.4 10.6 %collective-permute-start.9 = (f32[2,1,32,256]{3,1,2,0:T(1,128)S(1)}, f32[2,1,32,256]{3,1,2,0:T(1,128)S(1)}, u32[]{:S(2)}, u32[]{:S(2)}) collective-permute-start(f32[2,1,32,256]{3,1,2,0:T(1,128)S(1)} %get-tuple-element.67), channel_id=1, source_target_pairs={{0,8},{8,16},{16,24},{1,9},{9,17},{17,25},{2,10},{10,18},{18,26},{... | collective-permute-start | bytes 196616 | tf_op jit(solution)/shard_map/ppermute | solution.py:16
  53.3 12.5 %collective-permute-start.18 = (f32[4,34,1,256]{3,1,2,0:T(8,128)S(1)}, f32[4,34,1,256]{3,1,2,0:T(8,128)S(1)}, u32[]{:S(2)}, u32[]{:S(2)}) collective-permute-start(f32[4,34,1,256]{3,1,2,0:T(8,128)S(1)} %copy.49), channel_id=1, source_target_pairs={{0,1},{1,2},{2,3},{3,4},{4,5},{5,6},{6,7},{8,9},{9,10},{10,11},{11... | collective-permute-start | bytes 417800 | tf_op jit(solution)/shard_map/ppermute | solution.py:16
  57.8 8.2 %collective-permute-start.19 = (f32[4,34,1,256]{3,1,2,0:T(8,128)S(1)}, f32[4,34,1,256]{3,1,2,0:T(8,128)S(1)}, u32[]{:S(2)}, u32[]{:S(2)}) collective-permute-start(f32[4,34,1,256]{3,1,2,0:T(8,128)S(1)} %copy.50), channel_id=1, source_target_pairs={{1,0},{2,1},{3,2},{4,3},{5,4},{6,5},{7,6},{9,8},{10,9},{11,10},{12... | collective-permute-start | bytes 417800 | tf_op jit(solution)/shard_map/ppermute | solution.py:17
  59.1 7.1 %collective-permute-start.10 = (f32[2,34,1,256]{3,1,2,0:T(8,128)S(1)}, f32[2,34,1,256]{3,1,2,0:T(8,128)S(1)}, u32[]{:S(2)}, u32[]{:S(2)}) collective-permute-start(f32[2,34,1,256]{3,1,2,0:T(8,128)S(1)} %get-tuple-element.43), channel_id=1, source_target_pairs={{1,0},{2,1},{3,2},{4,3},{5,4},{6,5},{7,6},{9,8},{10,9},{11,10},{12... | collective-permute-start | bytes 208904 | tf_op jit(solution)/shard_map/ppermute | solution.py:17
  60.4 7.9 %collective-permute-start.11 = (f32[2,34,1,256]{3,1,2,0:T(8,128)S(1)}, f32[2,34,1,256]{3,1,2,0:T(8,128)S(1)}, u32[]{:S(2)}, u32[]{:S(2)}) collective-permute-start(f32[2,34,1,256]{3,1,2,0:T(8,128)S(1)} %get-tuple-element.44), channel_id=1, source_target_pairs={{0,1},{1,2},{2,3},{3,4},{4,5},{5,6},{6,7},{8,9},{9,10},{10,11},{11... | collective-permute-start | bytes 208904 | tf_op jit(solution)/shard_map/ppermute | solution.py:16
  71.8 6.1 %collective-permute-start.12 = (f32[2,1,32,256]{3,1,2,0:T(1,128)S(1)}, f32[2,1,32,256]{3,1,2,0:T(1,128)S(1)}, u32[]{:S(2)}, u32[]{:S(2)}) collective-permute-start(f32[2,1,32,256]{3,1,2,0:T(1,128)S(1)} %get-tuple-element.66), channel_id=1, source_target_pairs={{8,0},{16,8},{24,16},{9,1},{17,9},{25,17},{10,2},{18,10},{26,18},{... | collective-permute-start | bytes 196616 | tf_op jit(solution)/shard_map/ppermute | solution.py:17
  73.1 5.6 %collective-permute-start.13 = (f32[2,1,32,256]{3,1,2,0:T(1,128)S(1)}, f32[2,1,32,256]{3,1,2,0:T(1,128)S(1)}, u32[]{:S(2)}, u32[]{:S(2)}) collective-permute-start(f32[2,1,32,256]{3,1,2,0:T(1,128)S(1)} %get-tuple-element.65), channel_id=1, source_target_pairs={{0,8},{8,16},{16,24},{1,9},{9,17},{17,25},{2,10},{10,18},{18,26},{... | collective-permute-start | bytes 196616 | tf_op jit(solution)/shard_map/ppermute | solution.py:16
  78.7 6.1 %collective-permute-start.14 = (f32[2,34,1,256]{3,1,2,0:T(8,128)S(1)}, f32[2,34,1,256]{3,1,2,0:T(8,128)S(1)}, u32[]{:S(2)}, u32[]{:S(2)}) collective-permute-start(f32[2,34,1,256]{3,1,2,0:T(8,128)S(1)} %get-tuple-element.41), channel_id=1, source_target_pairs={{1,0},{2,1},{3,2},{4,3},{5,4},{6,5},{7,6},{9,8},{10,9},{11,10},{12... | collective-permute-start | bytes 208904 | tf_op jit(solution)/shard_map/ppermute | solution.py:17
  80.0 5.9 %collective-permute-start.15 = (f32[2,34,1,256]{3,1,2,0:T(8,128)S(1)}, f32[2,34,1,256]{3,1,2,0:T(8,128)S(1)}, u32[]{:S(2)}, u32[]{:S(2)}) collective-permute-start(f32[2,34,1,256]{3,1,2,0:T(8,128)S(1)} %get-tuple-element.42), channel_id=1, source_target_pairs={{0,1},{1,2},{2,3},{3,4},{4,5},{5,6},{6,7},{8,9},{9,10},{10,11},{11... | collective-permute-start | bytes 208904 | tf_op jit(solution)/shard_map/ppermute | solution.py:16
  89.6 8.2 %collective-permute-start.20 = (f32[2,1,32,256]{3,1,2,0:T(1,128)S(1)}, f32[2,1,32,256]{3,1,2,0:T(1,128)S(1)}, u32[]{:S(2)}, u32[]{:S(2)}) collective-permute-start(f32[2,1,32,256]{3,1,2,0:T(1,128)S(1)} %get-tuple-element.63), channel_id=1, source_target_pairs={{0,8},{8,16},{16,24},{1,9},{9,17},{17,25},{2,10},{10,18},{18,26},{... | collective-permute-start | bytes 196616 | tf_op jit(solution)/shard_map/ppermute | solution.py:16
  93.3 5.0 %collective-permute-start.21 = (f32[2,1,32,256]{3,1,2,0:T(1,128)S(1)}, f32[2,1,32,256]{3,1,2,0:T(1,128)S(1)}, u32[]{:S(2)}, u32[]{:S(2)}) collective-permute-start(f32[2,1,32,256]{3,1,2,0:T(1,128)S(1)} %get-tuple-element.64), channel_id=1, source_target_pairs={{8,0},{16,8},{24,16},{9,1},{17,9},{25,17},{10,2},{18,10},{26,18},{... | collective-permute-start | bytes 196616 | tf_op jit(solution)/shard_map/ppermute | solution.py:17
  98.3 7.2 %collective-permute-start.22 = (f32[2,34,1,256]{3,1,2,0:T(8,128)S(1)}, f32[2,34,1,256]{3,1,2,0:T(8,128)S(1)}, u32[]{:S(2)}, u32[]{:S(2)}) collective-permute-start(f32[2,34,1,256]{3,1,2,0:T(8,128)S(1)} %get-tuple-element.39), channel_id=1, source_target_pairs={{0,1},{1,2},{2,3},{3,4},{4,5},{5,6},{6,7},{8,9},{9,10},{10,11},{11... | collective-permute-start | bytes 208904 | tf_op jit(solution)/shard_map/ppermute | solution.py:16
  102.6 6.4 %collective-permute-start.23 = (f32[2,34,1,256]{3,1,2,0:T(8,128)S(1)}, f32[2,34,1,256]{3,1,2,0:T(8,128)S(1)}, u32[]{:S(2)}, u32[]{:S(2)}) collective-permute-start(f32[2,34,1,256]{3,1,2,0:T(8,128)S(1)} %get-tuple-element.40), channel_id=1, source_target_pairs={{1,0},{2,1},{3,2},{4,3},{5,4},{6,5},{7,6},{9,8},{10,9},{11,10},{12... | collective-permute-start | bytes 208904 | tf_op jit(solution)/shard_map/ppermute | solution.py:17
  117.0 5.0 %collective-permute-start.25 = (f32[2,1,32,256]{3,1,2,0:T(1,128)S(1)}, f32[2,1,32,256]{3,1,2,0:T(1,128)S(1)}, u32[]{:S(2)}, u32[]{:S(2)}) collective-permute-start(f32[2,1,32,256]{3,1,2,0:T(1,128)S(1)} %get-tuple-element.62), channel_id=1, source_target_pairs={{8,0},{16,8},{24,16},{9,1},{17,9},{25,17},{10,2},{18,10},{26,18},{... | collective-permute-start | bytes 196616 | tf_op jit(solution)/shard_map/ppermute | solution.py:17
  122.1 7.6 %collective-permute-start.26 = (f32[2,34,1,256]{3,1,2,0:T(8,128)S(1)}, f32[2,34,1,256]{3,1,2,0:T(8,128)S(1)}, u32[]{:S(2)}, u32[]{:S(2)}) collective-permute-start(f32[2,34,1,256]{3,1,2,0:T(8,128)S(1)} %get-tuple-element.37), channel_id=1, source_target_pairs={{0,1},{1,2},{2,3},{3,4},{4,5},{5,6},{6,7},{8,9},{9,10},{10,11},{11... | collective-permute-start | bytes 208904 | tf_op jit(solution)/shard_map/ppermute | solution.py:16
  126.3 5.2 %collective-permute-start.27 = (f32[2,34,1,256]{3,1,2,0:T(8,128)S(1)}, f32[2,34,1,256]{3,1,2,0:T(8,128)S(1)}, u32[]{:S(2)}, u32[]{:S(2)}) collective-permute-start(f32[2,34,1,256]{3,1,2,0:T(8,128)S(1)} %get-tuple-element.38), channel_id=1, source_target_pairs={{1,0},{2,1},{3,2},{4,3},{5,4},{6,5},{7,6},{9,8},{10,9},{11,10},{12... | collective-permute-start | bytes 208904 | tf_op jit(solution)/shard_map/ppermute | solution.py:17
  139.4 5.2 %collective-permute-start.29 = (f32[2,1,32,256]{3,1,2,0:T(1,128)S(1)}, f32[2,1,32,256]{3,1,2,0:T(1,128)S(1)}, u32[]{:S(2)}, u32[]{:S(2)}) collective-permute-start(f32[2,1,32,256]{3,1,2,0:T(1,128)S(1)} %get-tuple-element.60), channel_id=1, source_target_pairs={{8,0},{16,8},{24,16},{9,1},{17,9},{25,17},{10,2},{18,10},{26,18},{... | collective-permute-start | bytes 196616 | tf_op jit(solution)/shard_map/ppermute | solution.py:17
  147.7 5.2 %collective-permute-start.31 = (f32[2,34,1,256]{3,1,2,0:T(8,128)S(1)}, f32[2,34,1,256]{3,1,2,0:T(8,128)S(1)}, u32[]{:S(2)}, u32[]{:S(2)}) collective-permute-start(f32[2,34,1,256]{3,1,2,0:T(8,128)S(1)} %get-tuple-element.36), channel_id=1, source_target_pairs={{1,0},{2,1},{3,2},{4,3},{5,4},{6,5},{7,6},{9,8},{10,9},{11,10},{12... | collective-permute-start | bytes 208904 | tf_op jit(solution)/shard_map/ppermute | solution.py:17
  165.1 6.0 %collective-permute-start.34 = (f32[2,34,1,256]{3,1,2,0:T(8,128)S(1)}, f32[2,34,1,256]{3,1,2,0:T(8,128)S(1)}, u32[]{:S(2)}, u32[]{:S(2)}) collective-permute-start(f32[2,34,1,256]{3,1,2,0:T(8,128)S(1)} %get-tuple-element.33), channel_id=1, source_target_pairs={{0,1},{1,2},{2,3},{3,4},{4,5},{5,6},{6,7},{8,9},{9,10},{10,11},{11... | collective-permute-start | bytes 208904 | tf_op jit(solution)/shard_map/ppermute | solution.py:16
  169.4 5.2 %collective-permute-start.35 = (f32[2,34,1,256]{3,1,2,0:T(8,128)S(1)}, f32[2,34,1,256]{3,1,2,0:T(8,128)S(1)}, u32[]{:S(2)}, u32[]{:S(2)}) collective-permute-start(f32[2,34,1,256]{3,1,2,0:T(8,128)S(1)} %get-tuple-element.34), channel_id=1, source_target_pairs={{1,0},{2,1},{3,2},{4,3},{5,4},{6,5},{7,6},{9,8},{10,9},{11,10},{12... | collective-permute-start | bytes 208904 | tf_op jit(solution)/shard_map/ppermute | solution.py:17
  177.8 5.3 %collective-permute-start.36 = (f32[2,1,32,256]{3,1,2,0:T(1,128)S(1)}, f32[2,1,32,256]{3,1,2,0:T(1,128)S(1)}, u32[]{:S(2)}, u32[]{:S(2)}) collective-permute-start(f32[2,1,32,256]{3,1,2,0:T(1,128)S(1)} %get-tuple-element.56), channel_id=1, source_target_pairs={{8,0},{16,8},{24,16},{9,1},{17,9},{25,17},{10,2},{18,10},{26,18},{... | collective-permute-start | bytes 196616 | tf_op jit(solution)/shard_map/ppermute | solution.py:17
  179.1 5.3 %collective-permute-start.37 = (f32[2,1,32,256]{3,1,2,0:T(1,128)S(1)}, f32[2,1,32,256]{3,1,2,0:T(1,128)S(1)}, u32[]{:S(2)}, u32[]{:S(2)}) collective-permute-start(f32[2,1,32,256]{3,1,2,0:T(1,128)S(1)} %get-tuple-element.55), channel_id=1, source_target_pairs={{0,8},{8,16},{16,24},{1,9},{9,17},{17,25},{2,10},{10,18},{18,26},{... | collective-permute-start | bytes 196616 | tf_op jit(solution)/shard_map/ppermute | solution.py:16
  184.5 5.3 %collective-permute-start.38 = (f32[2,34,1,256]{3,1,2,0:T(8,128)S(1)}, f32[2,34,1,256]{3,1,2,0:T(8,128)S(1)}, u32[]{:S(2)}, u32[]{:S(2)}) collective-permute-start(f32[2,34,1,256]{3,1,2,0:T(8,128)S(1)} %get-tuple-element.31), channel_id=1, source_target_pairs={{1,0},{2,1},{3,2},{4,3},{5,4},{6,5},{7,6},{9,8},{10,9},{11,10},{12... | collective-permute-start | bytes 208904 | tf_op jit(solution)/shard_map/ppermute | solution.py:17
  185.8 6.2 %collective-permute-start.39 = (f32[2,34,1,256]{3,1,2,0:T(8,128)S(1)}, f32[2,34,1,256]{3,1,2,0:T(8,128)S(1)}, u32[]{:S(2)}, u32[]{:S(2)}) collective-permute-start(f32[2,34,1,256]{3,1,2,0:T(8,128)S(1)} %get-tuple-element.32), channel_id=1, source_target_pairs={{0,1},{1,2},{2,3},{3,4},{4,5},{5,6},{6,7},{8,9},{9,10},{10,11},{11... | collective-permute-start | bytes 208904 | tf_op jit(solution)/shard_map/ppermute | solution.py:16
  195.5 5.3 %collective-permute-start.40 = (f32[2,1,32,256]{3,1,2,0:T(1,128)S(1)}, f32[2,1,32,256]{3,1,2,0:T(1,128)S(1)}, u32[]{:S(2)}, u32[]{:S(2)}) collective-permute-start(f32[2,1,32,256]{3,1,2,0:T(1,128)S(1)} %get-tuple-element.54), channel_id=1, source_target_pairs={{8,0},{16,8},{24,16},{9,1},{17,9},{25,17},{10,2},{18,10},{26,18},{... | collective-permute-start | bytes 196616 | tf_op jit(solution)/shard_map/ppermute | solution.py:17
  196.8 5.3 %collective-permute-start.41 = (f32[2,1,32,256]{3,1,2,0:T(1,128)S(1)}, f32[2,1,32,256]{3,1,2,0:T(1,128)S(1)}, u32[]{:S(2)}, u32[]{:S(2)}) collective-permute-start(f32[2,1,32,256]{3,1,2,0:T(1,128)S(1)} %get-tuple-element.53), channel_id=1, source_target_pairs={{0,8},{8,16},{16,24},{1,9},{9,17},{17,25},{2,10},{10,18},{18,26},{... | collective-permute-start | bytes 196616 | tf_op jit(solution)/shard_map/ppermute | solution.py:16
  202.2 5.8 %collective-permute-start.42 = (f32[2,34,1,256]{3,1,2,0:T(8,128)S(1)}, f32[2,34,1,256]{3,1,2,0:T(8,128)S(1)}, u32[]{:S(2)}, u32[]{:S(2)}) collective-permute-start(f32[2,34,1,256]{3,1,2,0:T(8,128)S(1)} %get-tuple-element.29), channel_id=1, source_target_pairs={{1,0},{2,1},{3,2},{4,3},{5,4},{6,5},{7,6},{9,8},{10,9},{11,10},{12... | collective-permute-start | bytes 208904 | tf_op jit(solution)/shard_map/ppermute | solution.py:17
  203.5 7.0 %collective-permute-start.43 = (f32[2,34,1,256]{3,1,2,0:T(8,128)S(1)}, f32[2,34,1,256]{3,1,2,0:T(8,128)S(1)}, u32[]{:S(2)}, u32[]{:S(2)}) collective-permute-start(f32[2,34,1,256]{3,1,2,0:T(8,128)S(1)} %get-tuple-element.30), channel_id=1, source_target_pairs={{0,1},{1,2},{2,3},{3,4},{4,5},{5,6},{6,7},{8,9},{9,10},{10,11},{11... | collective-permute-start | bytes 208904 | tf_op jit(solution)/shard_map/ppermute | solution.py:16
  214.0 5.8 %collective-permute-start.44 = (f32[2,1,32,256]{3,1,2,0:T(1,128)S(1)}, f32[2,1,32,256]{3,1,2,0:T(1,128)S(1)}, u32[]{:S(2)}, u32[]{:S(2)}) collective-permute-start(f32[2,1,32,256]{3,1,2,0:T(1,128)S(1)} %get-tuple-element.52), channel_id=1, source_target_pairs={{8,0},{16,8},{24,16},{9,1},{17,9},{25,17},{10,2},{18,10},{26,18},{... | collective-permute-start | bytes 196616 | tf_op jit(solution)/shard_map/ppermute | solution.py:17
  215.3 5.8 %collective-permute-start.45 = (f32[2,1,32,256]{3,1,2,0:T(1,128)S(1)}, f32[2,1,32,256]{3,1,2,0:T(1,128)S(1)}, u32[]{:S(2)}, u32[]{:S(2)}) collective-permute-start(f32[2,1,32,256]{3,1,2,0:T(1,128)S(1)} %get-tuple-element.51), channel_id=1, source_target_pairs={{0,8},{8,16},{16,24},{1,9},{9,17},{17,25},{2,10},{10,18},{18,26},{... | collective-permute-start | bytes 196616 | tf_op jit(solution)/shard_map/ppermute | solution.py:16
  221.1 5.8 %collective-permute-start.46 = (f32[2,34,1,256]{3,1,2,0:T(8,128)S(1)}, f32[2,34,1,256]{3,1,2,0:T(8,128)S(1)}, u32[]{:S(2)}, u32[]{:S(2)}) collective-permute-start(f32[2,34,1,256]{3,1,2,0:T(8,128)S(1)} %get-tuple-element.27), channel_id=1, source_target_pairs={{1,0},{2,1},{3,2},{4,3},{5,4},{6,5},{7,6},{9,8},{10,9},{11,10},{12... | collective-permute-start | bytes 208904 | tf_op jit(solution)/shard_map/ppermute | solution.py:17
  222.4 5.9 %collective-permute-start.47 = (f32[2,34,1,256]{3,1,2,0:T(8,128)S(1)}, f32[2,34,1,256]{3,1,2,0:T(8,128)S(1)}, u32[]{:S(2)}, u32[]{:S(2)}) collective-permute-start(f32[2,34,1,256]{3,1,2,0:T(8,128)S(1)} %get-tuple-element.28), channel_id=1, source_target_pairs={{0,1},{1,2},{2,3},{3,4},{4,5},{5,6},{6,7},{8,9},{9,10},{10,11},{11... | collective-permute-start | bytes 208904 | tf_op jit(solution)/shard_map/ppermute | solution.py:16
  231.7 6.1 %collective-permute-start.48 = (f32[2,1,32,256]{3,1,2,0:T(1,128)S(1)}, f32[2,1,32,256]{3,1,2,0:T(1,128)S(1)}, u32[]{:S(2)}, u32[]{:S(2)}) collective-permute-start(f32[2,1,32,256]{3,1,2,0:T(1,128)S(1)} %get-tuple-element.50), channel_id=1, source_target_pairs={{8,0},{16,8},{24,16},{9,1},{17,9},{25,17},{10,2},{18,10},{26,18},{... | collective-permute-start | bytes 196616 | tf_op jit(solution)/shard_map/ppermute | solution.py:17
  233.2 5.9 %collective-permute-start.49 = (f32[2,1,32,256]{3,1,2,0:T(1,128)S(1)}, f32[2,1,32,256]{3,1,2,0:T(1,128)S(1)}, u32[]{:S(2)}, u32[]{:S(2)}) collective-permute-start(f32[2,1,32,256]{3,1,2,0:T(1,128)S(1)} %get-tuple-element.49), channel_id=1, source_target_pairs={{0,8},{8,16},{16,24},{1,9},{9,17},{17,25},{2,10},{10,18},{18,26},{... | collective-permute-start | bytes 196616 | tf_op jit(solution)/shard_map/ppermute | solution.py:16
  239.1 7.5 %collective-permute-start.50 = (f32[2,34,1,256]{3,1,2,0:T(8,128)S(1)}, f32[2,34,1,256]{3,1,2,0:T(8,128)S(1)}, u32[]{:S(2)}, u32[]{:S(2)}) collective-permute-start(f32[2,34,1,256]{3,1,2,0:T(8,128)S(1)} %get-tuple-element.25), channel_id=1, source_target_pairs={{1,0},{2,1},{3,2},{4,3},{5,4},{6,5},{7,6},{9,8},{10,9},{11,10},{12... | collective-permute-start | bytes 208904 | tf_op jit(solution)/shard_map/ppermute | solution.py:17
  240.4 6.7 %collective-permute-start.51 = (f32[2,34,1,256]{3,1,2,0:T(8,128)S(1)}, f32[2,34,1,256]{3,1,2,0:T(8,128)S(1)}, u32[]{:S(2)}, u32[]{:S(2)}) collective-permute-start(f32[2,34,1,256]{3,1,2,0:T(8,128)S(1)} %get-tuple-element.26), channel_id=1, source_target_pairs={{0,1},{1,2},{2,3},{3,4},{4,5},{5,6},{6,7},{8,9},{9,10},{10,11},{11... | collective-permute-start | bytes 208904 | tf_op jit(solution)/shard_map/ppermute | solution.py:16
  439.6 30.3 %all-to-all-start.1 = ((f32[8,8,32,256]{3,2,1,0:T(8,128)}), f32[8,8,32,256]{3,2,1,0:T(8,128)S(1)}, u32[]{:S(2)}, u32[]{:S(2)}) async-start(f32[8,8,32,256]{3,2,1,0:T(8,128)} %copy.62), calls=%async_computation.1 | async-start | bytes 4194304 | tf_op jit(solution)/shard_map/all_to_all | solution.py:105
  (10 other events, 68.4 us)
where the time goes:
time: 481 us; the launch traced here: 472 us
  blocking collectives  152 us (32%)
  starting transfers between devices  147 us (31%)
  waiting for transfers between devices  66.8 us (14%)
  other arithmetic  53 us (11%)
  local copies, waits for them, and re-layouts  31.4 us (7%)
  matrix products  18.7 us (4%)
    ppermute x26, starting transfers between devices, extended(): before = lax.ppermute(last, axis, up)  109 us
    all_to_all x1, blocking collectives, shards(): lax.all_to_all(both, 'probe', split_axis=2, concat_axis=0, tiled=True)  79.6 us
    psum x1, blocking collectives, shards(): lax.psum(jnp.stack([partial_gram, partial_cross]), ('probe', 'sx', 'sy'))  72.6 us
    ppermute x26, starting transfers between devices, extended(): after = lax.ppermute(leading, axis, down)  34.3 us
    all_to_all x1, waiting for transfers between devices, shards(): lax.all_to_all(basis_slab.reshape(slabs[:, 0].shape), 'probe', split_axis...  25.3 us
    ppermute x26, waiting for transfers between devices, extended(): after = lax.ppermute(leading, axis, down)  24.1 us
    add x6, other arithmetic, forward_step(): result + (spread - 0.5 * cc[3]) * padded[..., 2:]  20.5 us
    ppermute x26, waiting for transfers between devices, extended(): before = lax.ppermute(last, axis, up)  17.3 us
  transfers between devices with their start and end apart: 53, of which 21 were waited for; matrix products, arithmetic and copies ran while one was open for 5% of the time, Pallas kernels for 0%

commit v1 on v0

--- a/solution.py
+++ b/solution.py
@@ -98,7 +98,12 @@
     flat_root = slabs[:, 1].reshape(count, -1)
     partial_gram = jnp.dot(flat, flat.T, precision=highest)
     partial_cross = jnp.dot(flat_root, flat_root.T, precision=highest)
-    sums = lax.psum(jnp.stack([partial_gram, partial_cross]), ("probe", "sx", "sy")) / ncells
+    sums = (
+        jnp.sum(
+            lax.all_gather(jnp.stack([partial_gram, partial_cross]), ("probe", "sx", "sy")), axis=0
+        )
+        / ncells
+    )
     gram, cross = (sums[0], sums[1])
     inverse = factor_inverse(gram, count)
     basis_slab = jnp.dot(inverse, flat, precision=highest)

time: 481 us -> 736 us (1.53)
  blocking collectives: 152 us -> 371 us
  starting transfers between devices: 147 us -> 183 us
    all_gather x0 -> x1, blocking collectives: none -> 292 us  [shards(): lax.all_gather(jnp.stack([partial_gram, partial_cross]), ('probe', 'sx',...]
    psum x1 -> x0, blocking collectives: 72.6 us -> none  [shards(): lax.psum(jnp.stack([partial_gram, partial_cross]), ('probe', 'sx', 'sy'))]
    all_to_all x1, starting transfers between devices: 4.14 us -> 39.9 us  [shards(): lax.all_to_all(basis_slab.reshape(slabs[:, 0].shape), 'probe', split_axis...]
  transfers between devices with their start and end apart: 53 -> 53, of which waited for: 21 -> 21; matrix products, arithmetic and copies ran while one was open for 5% -> 3% of each run, Pallas kernels for 0% -> 0%
where the time goes in v1:
time: 736 us; the launch traced here: 727 us
  blocking collectives  371 us (50%)
  starting transfers between devices  183 us (25%)
  waiting for transfers between devices  66.8 us (9%)
  other arithmetic  53.1 us (7%)
  local copies, waits for them, and re-layouts  31.4 us (4%)
  matrix products  18.7 us (3%)
    all_gather x1, blocking collectives, shards(): lax.all_gather(jnp.stack([partial_gram, partial_cross]), ('probe', 'sx',...  292 us
    ppermute x26, starting transfers between devices, extended(): before = lax.ppermute(last, axis, up)  109 us
    all_to_all x1, blocking collectives, shards(): lax.all_to_all(both, 'probe', split_axis=2, concat_axis=0, tiled=True)  79.6 us
    all_to_all x1, starting transfers between devices, shards(): lax.all_to_all(basis_slab.reshape(slabs[:, 0].shape), 'probe', split_axis...  39.9 us
    ppermute x26, starting transfers between devices, extended(): after = lax.ppermute(leading, axis, down)  34.3 us
    all_to_all x1, waiting for transfers between devices, shards(): lax.all_to_all(basis_slab.reshape(slabs[:, 0].shape), 'probe', split_axis...  25.3 us
    ppermute x26, waiting for transfers between devices, extended(): after = lax.ppermute(leading, axis, down)  24.1 us
    add x6, other arithmetic, forward_step(): result + (spread - 0.5 * cc[3]) * padded[..., 2:]  20.5 us
  transfers between devices with their start and end apart: 53, of which 21 were waited for; matrix products, arithmetic and copies ran while one was open for 3% of the time, Pallas kernels for 0%

profile of v1, /device:TPU:1, one launch (start us, length us, event | category | flops | bytes accessed | tf_op | source)
XLA Modules:
  0.0 726.6 jit_solution(2225357516169832131)
XLA Ops:
  3.0 4.6 collective-permute-start.1
  12.0 4.4 collective-permute-start.3
  21.8 3.5 fusion.10
  26.7 4.0 collective-permute-start.5
  33.3 4.9 collective-permute-start.7
  38.3 4.0 collective-permute-start.16
  43.6 3.5 fusion.14
  48.4 4.6 collective-permute-start.9
  53.3 4.4 collective-permute-start.18
  60.4 4.8 collective-permute-start.11
  68.3 3.4 fusion.18
  73.1 4.3 collective-permute-start.13
  80.0 4.4 collective-permute-start.15
  85.9 3.5 broadcast_multiply_fusion.3
  89.6 3.7 collective-permute-start.20
  98.3 4.3 collective-permute-start.22
  105.5 3.5 collective-permute-done.23
  109.5 3.9 broadcast_multiply_fusion.2
  113.5 3.5 collective-permute-start.24
  118.4 3.7 collective-permute-done.25
  122.1 4.3 collective-permute-start.26
  132.0 3.9 broadcast_multiply_fusion.1
  140.7 3.9 collective-permute-done.29
  149.4 3.5 collective-permute-done.31
  153.3 3.7 broadcast_multiply_fusion
  161.4 3.7 collective-permute-done.33
  165.1 4.3 collective-permute-start.34
  171.1 3.4 collective-permute-done.35
  179.1 4.0 collective-permute-start.37
  185.8 4.0 collective-permute-start.39
  192.0 3.4 fusion.27
  196.8 4.0 collective-permute-start.41
  203.5 4.4 collective-permute-start.43
  210.5 3.4 fusion.31
  215.3 4.4 collective-permute-start.45
  222.4 4.4 collective-permute-start.47
  233.2 4.6 collective-permute-start.49
  240.4 5.3 collective-permute-start.51
  247.1 3.5 fusion.41
  253.3 79.6 %all_to_all.36 = f32[2,2,32,32,256]{4,3,0,1,2:T(8,128)S(1)} all-to-all(f32[2,2,32,32,256]{4,3,0,1,2:T(8,128)S(1)} %copy.58), channel_id=1, replica_groups=mesh['probe'=4,'sx'=4,'sy'=8] {'probe'}, dimensions={2} | all-to-all | bytes 8388608 | tf_op jit(solution)/shard_map/all_to_all | solution.py:96
  333.0 5.2 copy.72
  338.2 6.1 all_to_all.29
  344.4 7.1 fusion.131
  351.5 7.1 fusion.134
  358.6 291.7 %all-gather = f32[256,8,8]{2,1,0:T(8,128)S(1)} all-gather(f32[2,8,8]{2,1,0:T(8,128)S(1)} %pad_maximum_fusion.117), channel_id=2, replica_groups=mesh['probe'=4,'sx'=4,'sy'=8] {'probe','sx','sy'}, dimensions={0}, use_global_device_ids=true | all-gather | bytes 66048 | tf_op jit(solution)/shard_map/all_gather | solution.py:103
  653.4 3.4 fusion.124
  658.7 39.9 %all-to-all-start.1 = ((f32[8,8,32,256]{3,2,1,0:T(8,128)}), f32[8,8,32,256]{3,2,1,0:T(8,128)S(1)}, u32[]{:S(2)}, u32[]{:S(2)}) async-start(f32[8,8,32,256]{3,2,1,0:T(8,128)} %copy.62), calls=%async_computation.1 | async-start | bytes 4194304 | tf_op jit(solution)/shard_map/all_to_all | solution.py:110
  699.5 25.3 %all-to-all-done.1 = f32[8,8,32,256]{3,2,1,0:T(8,128)S(1)} async-done(((f32[8,8,32,256]{3,2,1,0:T(8,128)}), f32[8,8,32,256]{3,2,1,0:T(8,128)S(1)}, u32[]{:S(2)}, u32[]{:S(2)}) %all-to-all-start.1) | async-done | bytes 2097184 | tf_op jit(solution)/shard_map/all_to_all | solution.py:110
  (168 shorter events, 101.9 us)
Async XLA Ops:
  1.6 8.9 %collective-permute-start = (f32[2,1,32,256]{3,1,2,0:T(1,128)S(1)}, f32[2,1,32,256]{3,1,2,0:T(1,128)S(1)}, u32[]{:S(2)}, u32[]{:S(2)}) collective-permute-start(f32[2,1,32,256]{3,1,2,0:T(1,128)S(1)} %copy.38), channel_id=1, source_target_pairs={{8,0},{16,8},{24,16},{9,1},{17,9},{25,17},{10,2},{18,10},{26,18},{... | collective-permute-start | bytes 196616 | tf_op jit(solution)/shard_map/ppermute | solution.py:17
  3.0 7.6 %collective-permute-start.1 = (f32[2,1,32,256]{3,1,2,0:T(1,128)S(1)}, f32[2,1,32,256]{3,1,2,0:T(1,128)S(1)}, u32[]{:S(2)}, u32[]{:S(2)}) collective-permute-start(f32[2,1,32,256]{3,1,2,0:T(1,128)S(1)} %copy.41), channel_id=1, source_target_pairs={{0,8},{8,16},{16,24},{1,9},{9,17},{17,25},{2,10},{10,18},{18,26},{... | collective-permute-start | bytes 196616 | tf_op jit(solution)/shard_map/ppermute | solution.py:16
  10.6 11.2 %collective-permute-start.2 = (f32[2,34,1,256]{3,1,2,0:T(8,128)S(1)}, f32[2,34,1,256]{3,1,2,0:T(8,128)S(1)}, u32[]{:S(2)}, u32[]{:S(2)}) collective-permute-start(f32[2,34,1,256]{3,1,2,0:T(8,128)S(1)} %get-tuple-element.47), channel_id=1, source_target_pairs={{1,0},{2,1},{3,2},{4,3},{5,4},{6,5},{7,6},{9,8},{10,9},{11,10},{12... | collective-permute-start | bytes 208904 | tf_op jit(solution)/shard_map/ppermute | solution.py:17
  12.0 9.8 %collective-permute-start.3 = (f32[2,34,1,256]{3,1,2,0:T(8,128)S(1)}, f32[2,34,1,256]{3,1,2,0:T(8,128)S(1)}, u32[]{:S(2)}, u32[]{:S(2)}) collective-permute-start(f32[2,34,1,256]{3,1,2,0:T(8,128)S(1)} %get-tuple-element.48), channel_id=1, source_target_pairs={{0,1},{1,2},{2,3},{3,4},{4,5},{5,6},{6,7},{8,9},{9,10},{10,11},{11... | collective-permute-start | bytes 208904 | tf_op jit(solution)/shard_map/ppermute | solution.py:16
  25.4 5.3 collective-permute-start.4
  26.7 5.3 collective-permute-start.5
  32.0 11.5 %collective-permute-start.6 = (f32[2,34,1,256]{3,1,2,0:T(8,128)S(1)}, f32[2,34,1,256]{3,1,2,0:T(8,128)S(1)}, u32[]{:S(2)}, u32[]{:S(2)}) collective-permute-start(f32[2,34,1,256]{3,1,2,0:T(8,128)S(1)} %get-tuple-element.45), channel_id=1, source_target_pairs={{1,0},{2,1},{3,2},{4,3},{5,4},{6,5},{7,6},{9,8},{10,9},{11,10},{12... | collective-permute-start | bytes 208904 | tf_op jit(solution)/shard_map/ppermute | solution.py:17
  33.3 10.2 %collective-permute-start.7 = (f32[2,34,1,256]{3,1,2,0:T(8,128)S(1)}, f32[2,34,1,256]{3,1,2,0:T(8,128)S(1)}, u32[]{:S(2)}, u32[]{:S(2)}) collective-permute-start(f32[2,34,1,256]{3,1,2,0:T(8,128)S(1)} %get-tuple-element.46), channel_id=1, source_target_pairs={{0,1},{1,2},{2,3},{3,4},{4,5},{5,6},{6,7},{8,9},{9,10},{10,11},{11... | collective-permute-start | bytes 208904 | tf_op jit(solution)/shard_map/ppermute | solution.py:16
  38.3 14.8 %collective-permute-start.16 = (f32[4,1,32,256]{3,2,1,0:T(8,128)S(1)}, f32[4,1,32,256]{3,2,1,0:T(8,128)S(1)}, u32[]{:S(2)}, u32[]{:S(2)}) collective-permute-start(f32[4,1,32,256]{3,2,1,0:T(8,128)S(1)} %get-tuple-element.17), channel_id=1, source_target_pairs={{0,8},{8,16},{16,24},{1,9},{9,17},{17,25},{2,10},{10,18},{18,26},{... | collective-permute-start | bytes 393224 | tf_op jit(solution)/shard_map/ppermute | solution.py:16
  42.3 10.8 %collective-permute-start.17 = (f32[4,1,32,256]{3,2,1,0:T(8,128)S(1)}, f32[4,1,32,256]{3,2,1,0:T(8,128)S(1)}, u32[]{:S(2)}, u32[]{:S(2)}) collective-permute-start(f32[4,1,32,256]{3,2,1,0:T(8,128)S(1)} %get-tuple-element.18), channel_id=1, source_target_pairs={{8,0},{16,8},{24,16},{9,1},{17,9},{25,17},{10,2},{18,10},{26,18},{... | collective-permute-start | bytes 393224 | tf_op jit(solution)/shard_map/ppermute | solution.py:17
  47.1 11.9 %collective-permute-start.8 = (f32[2,1,32,256]{3,1,2,0:T(1,128)S(1)}, f32[2,1,32,256]{3,1,2,0:T(1,128)S(1)}, u32[]{:S(2)}, u32[]{:S(2)}) collective-permute-start(f32[2,1,32,256]{3,1,2,0:T(1,128)S(1)} %get-tuple-element.68), channel_id=1, source_target_pairs={{8,0},{16,8},{24,16},{9,1},{17,9},{25,17},{10,2},{18,10},{26,18},{... | collective-permute-start | bytes 196616 | tf_op jit(solution)/shard_map/ppermute | solution.py:17
  48.4 10.6 %collective-permute-start.9 = (f32[2,1,32,256]{3,1,2,0:T(1,128)S(1)}, f32[2,1,32,256]{3,1,2,0:T(1,128)S(1)}, u32[]{:S(2)}, u32[]{:S(2)}) collective-permute-start(f32[2,1,32,256]{3,1,2,0:T(1,128)S(1)} %get-tuple-element.67), channel_id=1, source_target_pairs={{0,8},{8,16},{16,24},{1,9},{9,17},{17,25},{2,10},{10,18},{18,26},{... | collective-permute-start | bytes 196616 | tf_op jit(solution)/shard_map/ppermute | solution.py:16
  53.3 12.5 %collective-permute-start.18 = (f32[4,34,1,256]{3,1,2,0:T(8,128)S(1)}, f32[4,34,1,256]{3,1,2,0:T(8,128)S(1)}, u32[]{:S(2)}, u32[]{:S(2)}) collective-permute-start(f32[4,34,1,256]{3,1,2,0:T(8,128)S(1)} %copy.49), channel_id=1, source_target_pairs={{0,1},{1,2},{2,3},{3,4},{4,5},{5,6},{6,7},{8,9},{9,10},{10,11},{11... | collective-permute-start | bytes 417800 | tf_op jit(solution)/shard_map/ppermute | solution.py:16
  57.8 8.2 %collective-permute-start.19 = (f32[4,34,1,256]{3,1,2,0:T(8,128)S(1)}, f32[4,34,1,256]{3,1,2,0:T(8,128)S(1)}, u32[]{:S(2)}, u32[]{:S(2)}) collective-permute-start(f32[4,34,1,256]{3,1,2,0:T(8,128)S(1)} %copy.50), channel_id=1, source_target_pairs={{1,0},{2,1},{3,2},{4,3},{5,4},{6,5},{7,6},{9,8},{10,9},{11,10},{12... | collective-permute-start | bytes 417800 | tf_op jit(solution)/shard_map/ppermute | solution.py:17
  59.1 7.1 collective-permute-start.10
  60.4 7.9 %collective-permute-start.11 = (f32[2,34,1,256]{3,1,2,0:T(8,128)S(1)}, f32[2,34,1,256]{3,1,2,0:T(8,128)S(1)}, u32[]{:S(2)}, u32[]{:S(2)}) collective-permute-start(f32[2,34,1,256]{3,1,2,0:T(8,128)S(1)} %get-tuple-element.44), channel_id=1, source_target_pairs={{0,1},{1,2},{2,3},{3,4},{4,5},{5,6},{6,7},{8,9},{9,10},{10,11},{11... | collective-permute-start | bytes 208904 | tf_op jit(solution)/shard_map/ppermute | solution.py:16
  71.8 6.1 collective-permute-start.12
  73.1 5.6 collective-permute-start.13
  78.7 6.1 collective-permute-start.14
  80.0 5.9 collective-permute-start.15
  89.6 8.2 %collective-permute-start.20 = (f32[2,1,32,256]{3,1,2,0:T(1,128)S(1)}, f32[2,1,32,256]{3,1,2,0:T(1,128)S(1)}, u32[]{:S(2)}, u32[]{:S(2)}) collective-permute-start(f32[2,1,32,256]{3,1,2,0:T(1,128)S(1)} %get-tuple-element.63), channel_id=1, source_target_pairs={{0,8},{8,16},{16,24},{1,9},{9,17},{17,25},{2,10},{10,18},{18,26},{... | collective-permute-start | bytes 196616 | tf_op jit(solution)/shard_map/ppermute | solution.py:16
  93.3 5.0 collective-permute-start.21
  98.3 7.2 collective-permute-start.22
  102.6 6.4 collective-permute-start.23
  117.0 5.0 collective-permute-start.25
  122.1 7.6 %collective-permute-start.26 = (f32[2,34,1,256]{3,1,2,0:T(8,128)S(1)}, f32[2,34,1,256]{3,1,2,0:T(8,128)S(1)}, u32[]{:S(2)}, u32[]{:S(2)}) collective-permute-start(f32[2,34,1,256]{3,1,2,0:T(8,128)S(1)} %get-tuple-element.37), channel_id=1, source_target_pairs={{0,1},{1,2},{2,3},{3,4},{4,5},{5,6},{6,7},{8,9},{9,10},{10,11},{11... | collective-permute-start | bytes 208904 | tf_op jit(solution)/shard_map/ppermute | solution.py:16
  126.3 5.2 collective-permute-start.27
  139.4 5.2 collective-permute-start.29
  147.7 5.2 collective-permute-start.31
  165.1 6.0 collective-permute-start.34
  169.4 5.2 collective-permute-start.35
  177.8 5.3 collective-permute-start.36
  179.1 5.3 collective-permute-start.37
  184.5 5.3 collective-permute-start.38
  185.8 6.2 collective-permute-start.39
  195.5 5.3 collective-permute-start.40
  196.8 5.3 collective-permute-start.41
  202.2 5.8 collective-permute-start.42
  203.5 7.0 collective-permute-start.43
  214.0 5.8 collective-permute-start.44
  215.3 5.8 collective-permute-start.45
  221.1 5.8 collective-permute-start.46
  222.4 5.9 collective-permute-start.47
  231.7 6.1 collective-permute-start.48
  233.2 5.9 collective-permute-start.49
  239.1 7.5 %collective-permute-start.50 = (f32[2,34,1,256]{3,1,2,0:T(8,128)S(1)}, f32[2,34,1,256]{3,1,2,0:T(8,128)S(1)}, u32[]{:S(2)}, u32[]{:S(2)}) collective-permute-start(f32[2,34,1,256]{3,1,2,0:T(8,128)S(1)} %get-tuple-element.25), channel_id=1, source_target_pairs={{1,0},{2,1},{3,2},{4,3},{5,4},{6,5},{7,6},{9,8},{10,9},{11,10},{12... | collective-permute-start | bytes 208904 | tf_op jit(solution)/shard_map/ppermute | solution.py:17
  240.4 6.7 collective-permute-start.51
  658.7 66.1 %all-to-all-start.1 = ((f32[8,8,32,256]{3,2,1,0:T(8,128)}), f32[8,8,32,256]{3,2,1,0:T(8,128)S(1)}, u32[]{:S(2)}, u32[]{:S(2)}) async-start(f32[8,8,32,256]{3,2,1,0:T(8,128)} %copy.62), calls=%async_computation.1 | async-start | bytes 4194304 | tf_op jit(solution)/shard_map/all_to_all | solution.py:110
  (10 other events, 68.4 us)
